TPU v7x, 512 devices: a whole 4x8x8 slice. The times are simulated.
512 devices in a mesh: rows: 64 (over x, z, core), cols: 8 (over y).
Axes of the slice: x: 4, y: 8, z: 8, core: 2. Of those that a mesh axis runs over, the one named last changes fastest.
Arguments:
- right_sides: float32 [4, 64, 128, 256], P(None, 'rows'), may hold values from -6 to 6
- factor_blocks: bfloat16 [3, 64, 8, 8, 256, 256], P(None, 'rows', 'cols'), may hold values from -0.125 to 0.125
- diag_inverses: bfloat16 [4, 64, 256, 256], P(None, 'rows')
- source_ids: int32 [3, 64, 8, 8], P(None, 'rows', 'cols'), may hold values from 0 to 191, as said below
- block_counts: int32 [3, 64, 8], P(None, 'rows', 'cols'), may hold values from 1 to 8, as said below
Outputs:
- solution: float32 [4, 64, 128, 256], P(None, 'rows', 'cols')
Inputs may be any that keep to these rules, and one draw needn't show every extreme that they name: source_ids[l, t, c, k] = m * 64 + s names a supernode of a level m <= l with s % 8 == c. block_counts[l, t, c] slots of target t on group c hold blocks of the factor; slots at and past it are not part of the factor. In every level some target and group has all 8 slots live.
All inputs are finite; a program needn't handle non-finite values.
Results may differ from a plain program's by a relative error of at most 0.007.
Values may be sent and summed in bfloat16 or wider, within the bound.
A program may use at most 128 MiB of HBM per device.

v0:
```python
import jax
import jax.numpy as jnp
from jax import lax
from jax.sharding import PartitionSpec as P


def locate(source, row_count, col_count):
    return source // row_count * (row_count // col_count) + source % row_count // col_count


def slot_sum(running, blocks, chosen_ids, live_count, solved_store, row_count, col_count):

    def add_block(slot_index, partial_value):
        source = chosen_ids[slot_index]
        solved_piece = lax.dynamic_index_in_dim(
            solved_store, locate(source, row_count, col_count), 0, keepdims=False
        )
        factor_piece = lax.dynamic_index_in_dim(blocks, slot_index, 0, keepdims=False)
        return partial_value + jnp.dot(
            solved_piece, factor_piece, preferred_element_type=jnp.float32
        )

    return lax.fori_loop(0, live_count, add_block, running)


def shards(right_sides, factor_blocks, diag_inverses, source_ids, block_counts):
    row_count = lax.axis_size("rows")
    col_count = lax.axis_size("cols")
    level_count = right_sides.shape[0]
    rhs_count = right_sides.shape[2]
    block_width = right_sides.shape[3]
    share_rows = rhs_count // col_count
    col_index = lax.axis_index("cols")
    per_level = row_count // col_count
    solved_store = jnp.zeros(((level_count - 1) * per_level, rhs_count, block_width), jnp.bfloat16)
    partials = [jnp.zeros((rhs_count, block_width), jnp.float32)] * level_count
    solutions = []
    for level_index in range(level_count):
        if level_index > 0:
            partials[level_index] = slot_sum(
                partials[level_index],
                factor_blocks[level_index - 1, 0, 0],
                source_ids[level_index - 1, 0, 0],
                block_counts[level_index - 1, 0, 0],
                solved_store,
                row_count,
                col_count,
            )
        own_rhs = lax.dynamic_slice_in_dim(
            right_sides[level_index, 0], col_index * share_rows, share_rows, 0
        )
        if level_index > 0:
            own_rhs = own_rhs - lax.psum_scatter(
                partials[level_index], "cols", scatter_dimension=0, tiled=True
            )
        own_solution = jnp.dot(
            own_rhs.astype(jnp.bfloat16),
            diag_inverses[level_index, 0],
            preferred_element_type=jnp.float32,
        )
        solutions.append(own_solution)
        if level_index < level_count - 1:
            pieces = lax.all_gather(
                own_solution.astype(jnp.bfloat16)[None], "rows", axis=0, tiled=True
            )
            grouped = pieces.reshape(per_level, col_count, share_rows, block_width)
            regrouped = lax.all_to_all(grouped, "cols", split_axis=1, concat_axis=2, tiled=True)
            solved_store = solved_store.at[
                level_index * per_level : (level_index + 1) * per_level
            ].set(regrouped[:, 0])
    return jnp.stack(solutions)[:, None]


def solution(mesh):
    return jax.shard_map(
        shards,
        mesh=mesh,
        in_specs=(
            P(None, "rows", None, None),
            P(None, "rows", "cols", None, None, None),
            P(None, "rows", None, None),
            P(None, "rows", "cols", None),
            P(None, "rows", "cols"),
        ),
        out_specs=P(None, "rows", "cols", None),
        check_vma=False,
    )
```

profile of v0, /device:TPU:1, one launch (start us, length us, event | category | flops | bytes accessed | tf_op | source)
XLA Modules:
  0.0 457.7 jit_solution(18360709935676070336)
XLA Ops:
  6.5 0.9 slice.116
  7.5 1.0 fusion.40
  8.5 57.6 %all-gather = bf16[1024,256]{1,0:T(8,128)(2,1)S(1)} all-gather(bf16[16,256]{1,0:T(8,128)(2,1)S(1)} %get-tuple-element.425), channel_id=2, replica_groups=mesh['rows'=64,'cols'=8] {'rows'}, dimensions={0}, use_global_device_ids=true | all-gather | bytes 532480 | tf_op jit(solution)/shard_map/all_gather | solution.py:63
  66.2 0.8 copy.11
  67.0 6.8 %all-to-all-start = ((bf16[8,8,16,256]{3,2,0,1:T(8,128)(2,1)}), bf16[8,8,16,256]{3,2,0,1:T(8,128)(2,1)S(1)}, u32[]{:S(2)}, u32[]{:S(2)}) async-start(bf16[8,8,16,256]{3,2,0,1:T(8,128)(2,1)} %copy.11), calls=%async_computation | async-start | bytes 1048576 | tf_op jit(solution)/shard_map/all_to_all | solution.py:67
  75.1 3.5 slice_bitcast_fusion
  78.6 13.2 %all-to-all-done = bf16[8,8,16,256]{3,2,0,1:T(8,128)(2,1)S(1)} async-done(((bf16[8,8,16,256]{3,2,0,1:T(8,128)(2,1)}), bf16[8,8,16,256]{3,2,0,1:T(8,128)(2,1)S(1)}, u32[]{:S(2)}, u32[]{:S(2)}) %all-to-all-start) | async-done | bytes 524320 | tf_op jit(solution)/shard_map/all_to_all | solution.py:67
  92.0 21.2 %while.42 = (s32[]{:T(128)}, f32[128,256]{1,0:T(8,128)S(1)}, s32[]{:T(128)}, s32[8]{0:T(128)S(1)}, bf16[24,128,256]{2,1,0:T(8,128)(2,1)S(1)}, /*index=5*/bf16[8,...) while((s32[]{:T(128)}, f32[128,256]{1,0:T(8,128)S(1)}, ...), condition=%wide.region_1.2_spmd, body=%wide.region_0.0_spmd.sunk | while | flops 16810028 | bytes 459350 | solution.py:23
  92.7 0.7 dynamic_slice.141
  96.2 1.1 convolution_add_fusion.6
  97.8 0.7 dynamic_slice.141
  101.3 1.1 convolution_add_fusion.6
  103.0 0.7 dynamic_slice.141
  106.5 1.1 convolution_add_fusion.6
  111.6 1.1 convolution_add_fusion.6
  114.0 45.4 %reduce-scatter.4.cloned.1.call-done = f32[16,256]{1,0:T(8,128)} async-done(((f32[128,256]{1,0:T(8,128)}), f32[16,256]{1,0:T(8,128)}) %reduce-scatter.4.cloned.1.call-update) | async-done | bytes 16400 | tf_op jit(solution)/shard_map/reduce_scatter | solution.py:53
  159.4 1.1 fusion.41
  160.5 57.4 %all-gather.1 = bf16[1024,256]{1,0:T(8,128)(2,1)S(1)} all-gather(bf16[16,256]{1,0:T(8,128)(2,1)S(1)} %get-tuple-element.427), channel_id=3, replica_groups=mesh['rows'=64,'cols'=8] {'rows'}, dimensions={0}, use_global_device_ids=true | all-gather | bytes 532480 | tf_op jit(solution)/shard_map/all_gather | solution.py:63
  217.9 0.8 copy.13
  218.7 4.5 all-to-all-start.1
  223.2 17.9 %all-to-all-done.1 = bf16[8,8,16,256]{3,2,0,1:T(8,128)(2,1)S(1)} async-done(((bf16[8,8,16,256]{3,2,0,1:T(8,128)(2,1)}), bf16[8,8,16,256]{3,2,0,1:T(8,128)(2,1)S(1)}, u32[]{:S(2)}, u32[]{:S(2)}) %all-to-all-start.1) | async-done | bytes 524320 | tf_op jit(solution)/shard_map/all_to_all | solution.py:67
  241.3 5.6 %while.43 = (s32[]{:T(128)}, f32[128,256]{1,0:T(8,128)S(1)}, s32[]{:T(128)}, s32[8]{0:T(128)S(1)}, bf16[24,128,256]{2,1,0:T(8,128)(2,1)S(1)}, /*index=5*/bf16[8,...) while((s32[]{:T(128)}, f32[128,256]{1,0:T(8,128)S(1)}, ...), condition=%wide.region_4.5_spmd, body=%wide.region_3.4_spmd.sunk | while | flops 16810028 | bytes 459350 | solution.py:23
  245.2 1.1 convolution_add_fusion.7
  247.6 60.6 %reduce-scatter.6.cloned.1.call-done = f32[16,256]{1,0:T(8,128)} async-done(((f32[128,256]{1,0:T(8,128)}), f32[16,256]{1,0:T(8,128)}) %reduce-scatter.6.cloned.1.call-update) | async-done | bytes 16400 | tf_op jit(solution)/shard_map/reduce_scatter | solution.py:53
  308.2 1.1 fusion.42
  309.3 57.4 %all-gather.2 = bf16[1024,256]{1,0:T(8,128)(2,1)S(1)} all-gather(bf16[16,256]{1,0:T(8,128)(2,1)S(1)} %get-tuple-element.429), channel_id=4, replica_groups=mesh['rows'=64,'cols'=8] {'rows'}, dimensions={0}, use_global_device_ids=true | all-gather | bytes 532480 | tf_op jit(solution)/shard_map/all_gather | solution.py:63
  366.7 0.9 copy.15
  367.6 4.4 all-to-all-start.2
  372.0 17.9 %all-to-all-done.2 = bf16[8,8,16,256]{3,2,0,1:T(8,128)(2,1)S(1)} async-done(((bf16[8,8,16,256]{3,2,0,1:T(8,128)(2,1)}), bf16[8,8,16,256]{3,2,0,1:T(8,128)(2,1)S(1)}, u32[]{:S(2)}, u32[]{:S(2)}) %all-to-all-start.2) | async-done | bytes 524320 | tf_op jit(solution)/shard_map/all_to_all | solution.py:67
  390.0 4.6 %while.44 = (s32[]{:T(128)}, f32[128,256]{1,0:T(8,128)S(1)}, s32[]{:T(128)}, s32[8]{0:T(128)S(1)}, bf16[24,128,256]{2,1,0:T(8,128)(2,1)S(1)}, /*index=5*/bf16[8,...) while((s32[]{:T(128)}, f32[128,256]{1,0:T(8,128)S(1)}, ...), condition=%wide.region_7.8_spmd, body=%wide.region_6.7_spmd.sunk | while | flops 16810028 | bytes 459350 | solution.py:23
  395.3 54.2 %reduce-scatter.8.cloned.1.call-done = f32[16,256]{1,0:T(8,128)} async-done(((f32[128,256]{1,0:T(8,128)}), f32[16,256]{1,0:T(8,128)}) %reduce-scatter.8.cloned.1.call-update) | async-done | bytes 16400 | tf_op jit(solution)/shard_map/reduce_scatter | solution.py:53
  449.5 1.1 convolution_bitcast_fusion
  (39 shorter events, 6.4 us)
Async XLA Ops:
  6.5 67.3 %copy-start.4 = (s32[3,1,1]{0,2,1:T(1,128)S(1)}, s32[3,1,1]{0,2,1:T(1,128)}, u32[]{:S(2)}) copy-start(s32[3,1,1]{0,2,1:T(1,128)} %param.21) | copy-start | bytes 40
  6.5 68.0 %copy-start.5 = (s32[3,1,1,8]{3,2,1,0:T(1,128)S(1)}, s32[3,1,1,8]{3,2,1,0:T(1,128)}, u32[]{:S(2)}) copy-start(s32[3,1,1,8]{3,2,1,0:T(1,128)} %param.20) | copy-start | bytes 292
  67.0 24.8 %all-to-all-start = ((bf16[8,8,16,256]{3,2,0,1:T(8,128)(2,1)}), bf16[8,8,16,256]{3,2,0,1:T(8,128)(2,1)S(1)}, u32[]{:S(2)}, u32[]{:S(2)}) async-start(bf16[8,8,16,256]{3,2,0,1:T(8,128)(2,1)} %copy.11), calls=%async_computation | async-start | bytes 1048576 | tf_op jit(solution)/shard_map/all_to_all | solution.py:67
  73.8 85.6 %reduce-scatter.4.cloned.1.call-start = ((), (), s32[]{:S(2)}) async-start(), calls=%async_computation.6 | async-start | bytes 147456 | tf_op jit(solution)/shard_map/reduce_scatter | solution.py:53
  92.0 22.0 %copy-start.3 = (f32[4,1,128,256]{3,2,1,0:T(8,128)S(1)}, f32[4,1,128,256]{3,2,1,0:T(8,128)}, u32[]{:S(2)}) copy-start(f32[4,1,128,256]{3,2,1,0:T(8,128)} %param.17) | copy-start | bytes 1572868
  113.3 0.7 copy-start.1
  218.7 22.5 %copy-start.7 = (s32[8]{0:T(128)S(1)}, s32[8]{0:T(128)}, u32[]{:S(2)}) copy-start(s32[8]{0:T(128)} %get-tuple-element.596) | copy-start | bytes 100
  218.7 22.4 %all-to-all-start.1 = ((bf16[8,8,16,256]{3,2,0,1:T(8,128)(2,1)}), bf16[8,8,16,256]{3,2,0,1:T(8,128)(2,1)S(1)}, u32[]{:S(2)}, u32[]{:S(2)}) async-start(bf16[8,8,16,256]{3,2,0,1:T(8,128)(2,1)} %copy.13), calls=%async_computation.2 | async-start | bytes 1048576 | tf_op jit(solution)/shard_map/all_to_all | solution.py:67
  223.2 85.0 %reduce-scatter.6.cloned.1.call-start = ((), (), s32[]{:S(2)}) async-start(), calls=%async_computation.7 | async-start | bytes 147456 | tf_op jit(solution)/shard_map/reduce_scatter | solution.py:53
  246.9 0.6 copy-start.2
  367.6 22.5 %copy-start.6 = (s32[8]{0:T(128)S(1)}, s32[8]{0:T(128)}, u32[]{:S(2)}) copy-start(s32[8]{0:T(128)} %get-tuple-element.644) | copy-start | bytes 100
  367.6 22.3 %all-to-all-start.2 = ((bf16[8,8,16,256]{3,2,0,1:T(8,128)(2,1)}), bf16[8,8,16,256]{3,2,0,1:T(8,128)(2,1)S(1)}, u32[]{:S(2)}, u32[]{:S(2)}) async-start(bf16[8,8,16,256]{3,2,0,1:T(8,128)(2,1)} %copy.15), calls=%async_computation.4 | async-start | bytes 1048576 | tf_op jit(solution)/shard_map/all_to_all | solution.py:67
  371.9 77.5 %reduce-scatter.8.cloned.1.call-start = ((), (), s32[]{:S(2)}) async-start(), calls=%async_computation.8 | async-start | bytes 147456 | tf_op jit(solution)/shard_map/reduce_scatter | solution.py:53
  394.6 0.6 copy-start
Sparse Core Ops, SparseCore 0:
  114.1 45.2 reduce-scatter.3
  247.7 60.4 reduce-scatter.5
  395.4 54.0 reduce-scatter.7
where the time goes:
time: 464 us; the launch traced here: 458 us
  waiting for transfers between devices  209 us (45%)
  blocking collectives  172 us (37%)
  loops' own time  22 us (5%)
  starting transfers between devices  15.8 us (3%)
  local copies, waits for them, and re-layouts  14.4 us (3%)
  between operations  13.3 us (3%)
  matrix products  9.78 us (2%)
    all_gather x3, blocking collectives, shards(): lax.all_gather(own_solution.astype(jnp.bfloat16)[None], 'rows', axis=0, t...  172 us
    reduce_scatter x3, waiting for transfers between devices, shards(): lax.psum_scatter(partials[level_index], 'cols', scatter_dimension=0, tile...  160 us
    all_to_all x3, waiting for transfers between devices, shards(): lax.all_to_all(grouped, 'cols', split_axis=1, concat_axis=2, tiled=True)  49.1 us
    another operation x3, loops' own time, slot_sum(): return lax.fori_loop(0, live_count, add_block, running)  22 us
    all_to_all x3, starting transfers between devices, shards(): lax.all_to_all(grouped, 'cols', split_axis=1, concat_axis=2, tiled=True)  15.7 us
  transfers between devices with their start and end apart: 6, of which 6 were waited for; matrix products, arithmetic and copies ran while one was open for 1% of the time, Pallas kernels for 0%

commit v1 on v0

v1 whole, which is shorter than its diff:
```python
import jax
import jax.numpy as jnp
from jax import lax
from jax.experimental import pallas as pl
from jax.experimental.pallas import tpu as pltpu
from jax.sharding import PartitionSpec as P

LEV, NX, NZ, NC, NY = 4, 4, 8, 2, 8
W, RHS, BPD = 256, 128, 8
SHARE = RHS // NY
FAR8 = (4, 3, 5, 2, 6, 1, 7)
FAR4 = (2, 1, 3)
MESH = pl.DeviceIdType.MESH


def kernel(
    ids_ref, counts_ref, rhs_hbm, fac_hbm, diag_hbm, out_ref,
    store0, store1, store2, part, landed, rhs_full, rhs_own, fac, diag, piece,
    load_sem, r_send, r_recv, a_send, a_recv, b_send, b_recv, c_send, c_recv, d_send, d_recv,
):
    stores = (store0, store1, store2)
    row = lax.axis_index("rows")
    col = lax.axis_index("cols")
    x = row // (NZ * NC)
    z = (row // NC) % NZ
    core = row % NC
    root = row % NY
    src_core = col % NC
    in_lane = core == src_core
    is_root = root == col
    own_half = z // (NZ // 2)
    own_slot = 2 * x + own_half

    def rows_of(xx, zz, cc):
        return (xx * NZ + zz) * NC + cc

    own_rows = pl.ds(pl.multiple_of(col * SHARE, SHARE), SHARE)

    loads = [
        pltpu.make_async_copy(rhs_hbm.at[0, 0], rhs_full, load_sem.at[0]),
        pltpu.make_async_copy(diag_hbm.at[0, 0], diag.at[0], load_sem.at[1]),
        pltpu.make_async_copy(rhs_hbm.at[:, 0, own_rows, :], rhs_own, load_sem.at[2]),
    ]
    for level in range(1, LEV):
        loads.append(
            pltpu.make_async_copy(fac_hbm.at[level - 1, 0, 0], fac.at[level - 1], load_sem.at[1 + 2 * level])
        )
        loads.append(pltpu.make_async_copy(diag_hbm.at[level, 0], diag.at[level], load_sem.at[2 + 2 * level]))
    for copy in loads:
        copy.start()

    barrier = pltpu.get_barrier_semaphore()
    for d in FAR8:
        pl.semaphore_signal(barrier, device_id=(row, (col + d) % NY), device_id_type=MESH)
        pl.semaphore_signal(barrier, device_id=(rows_of(x, (z + d) % NZ, core), col), device_id_type=MESH)
    for d in FAR4:
        pl.semaphore_signal(barrier, device_id=(rows_of((x + d) % NX, z, core), col), device_id_type=MESH)
    pl.semaphore_signal(barrier, device_id=(rows_of(x, z, 1 - core), col), device_id_type=MESH)

    def r_copy(level, d):
        to = (col + d) % NY
        return pltpu.make_async_remote_copy(
            part.at[level - 1, pl.ds(pl.multiple_of(to * SHARE, SHARE), SHARE), :],
            landed.at[level - 1, d],
            r_send.at[level - 1, d],
            r_recv.at[level - 1, d],
            device_id=(row, to),
            device_id_type=MESH,
        )

    def a_copy(level):
        return pltpu.make_async_remote_copy(
            piece.at[level - 1],
            stores[level].at[own_slot, own_rows, :],
            a_send.at[level - 1],
            a_recv.at[level - 1, col],
            device_id=(row, root),
            device_id_type=MESH,
        )

    def a_wait(level, d):
        frm = (col + d) % NY
        pltpu.make_async_remote_copy(
            piece.at[level - 1],
            stores[level].at[own_slot, pl.ds(pl.multiple_of(frm * SHARE, SHARE), SHARE), :],
            a_send.at[level - 1],
            a_recv.at[level - 1, frm],
            device_id=(row, frm),
            device_id_type=MESH,
        ).wait_recv()

    def b_copy(level, half, d):
        slot = 2 * x + half
        return pltpu.make_async_remote_copy(
            stores[level].at[slot],
            stores[level].at[slot],
            b_send.at[level, d],
            b_recv.at[level, half],
            device_id=(rows_of(x, (z + d) % NZ, core), col),
            device_id_type=MESH,
        )

    def c_copy(level, from_x, half, d):
        slot = 2 * from_x + half
        return pltpu.make_async_remote_copy(
            stores[level].at[slot],
            stores[level].at[slot],
            c_send.at[level, d, half],
            c_recv.at[level, d, half],
            device_id=(rows_of((x + d) % NX, z, core), col),
            device_id_type=MESH,
        )

    def d_copy(level, slot):
        return pltpu.make_async_remote_copy(
            stores[level].at[slot],
            stores[level].at[slot],
            d_send.at[level, slot],
            d_recv.at[level, slot],
            device_id=(rows_of(x, z, 1 - core), col),
            device_id_type=MESH,
        )

    def relay(level, half):
        for d in FAR4:
            c_copy(level, x, half, d).start()
        d_copy(level, 2 * x + half).start()

    def spread(level):
        @pl.when(is_root)
        def _():
            if level > 0:
                for d in range(1, NY):
                    a_wait(level, d)
            for d in FAR8:
                b_copy(level, own_half, d).start()
            relay(level, own_half)

        @pl.when(in_lane)
        def _():
            for other in range(2):
                half = (own_half + 1 + other) % 2

                @pl.when(jnp.logical_not(jnp.logical_and(is_root, half == own_half)))
                def _():
                    b_copy(level, half, 1).wait_recv()
                    relay(level, half)

            for d in (1, 3, 2):
                from_x = (x + NX - d) % NX
                for half in range(2):
                    c_copy(level, from_x, half, d).wait_recv()
                    d_copy(level, 2 * from_x + half).start()

        @pl.when(jnp.logical_not(in_lane))
        def _():
            for slot in range(8):
                d_copy(level, slot).wait_recv()

    def drain(level):
        if level > 0:
            for d in FAR8:
                r_copy(level, d).wait_send()
        if level == LEV - 1:
            return
        if level > 0:

            @pl.when(jnp.logical_not(is_root))
            def _():
                a_copy(level).wait_send()

        @pl.when(is_root)
        def _():
            for d in FAR8:
                b_copy(level, own_half, d).wait_send()

        @pl.when(in_lane)
        def _():
            for half in range(2):
                for d in FAR4:
                    c_copy(level, x, half, d).wait_send()
            for slot in range(8):
                d_copy(level, slot).wait_send()

    loads[0].wait()
    loads[1].wait()

    @pl.when(is_root)
    def _():
        whole = jnp.dot(rhs_full[...].astype(jnp.bfloat16), diag[0], preferred_element_type=jnp.float32)
        store0[own_slot] = whole.astype(jnp.bfloat16)

    pl.semaphore_wait(barrier, 2 * (NY - 1) + NX)
    loads[2].wait()
    out_ref[0] = jnp.dot(rhs_own[0].astype(jnp.bfloat16), diag[0], preferred_element_type=jnp.float32)
    spread(0)

    for level in range(1, LEV):
        loads[1 + 2 * level].wait()
        loads[2 + 2 * level].wait()
        live = counts_ref[level - 1]
        total = jnp.zeros((RHS, W), jnp.float32)
        for k in range(BPD):
            source = ids_ref[(level - 1) * BPD + k]
            place = (source % (NX * NZ * NC)) // NY
            held = source // (NX * NZ * NC)
            block = store0[place]
            for m in range(1, level):
                block = lax.select(held == m, stores[m][place], block)
            block = lax.select(k < live, block, jnp.zeros_like(block))
            total = total + jnp.dot(block, fac[level - 1, k], preferred_element_type=jnp.float32)
        part[level - 1] = total
        for d in FAR8:
            r_copy(level, d).start()
        update = part[level - 1, own_rows, :]
        for d in (1, 7, 2, 6, 3, 5, 4):
            r_copy(level, d).wait_recv()
            update = update + landed[level - 1, d]
        reduced = (rhs_own[level] - update).astype(jnp.bfloat16)
        solved = jnp.dot(reduced, diag[level], preferred_element_type=jnp.float32)
        out_ref[level] = solved
        if level < LEV - 1:

            @pl.when(is_root)
            def _():
                stores[level][own_slot, own_rows, :] = solved.astype(jnp.bfloat16)

            @pl.when(jnp.logical_not(is_root))
            def _():
                piece[level - 1] = solved.astype(jnp.bfloat16)
                a_copy(level).start()

            spread(level)

    for level in range(LEV):
        drain(level)


def shards(right_sides, factor_blocks, diag_inverses, source_ids, block_counts):
    dma = pltpu.SemaphoreType.DMA
    hbm = pl.BlockSpec(memory_space=pl.ANY)
    smem = pl.BlockSpec(memory_space=pltpu.SMEM)
    store = pltpu.VMEM((8, RHS, W), jnp.bfloat16)
    out = pl.pallas_call(
        kernel,
        out_shape=jax.ShapeDtypeStruct((LEV, SHARE, W), jnp.float32),
        in_specs=[smem, smem, hbm, hbm, hbm],
        out_specs=pl.BlockSpec(memory_space=pltpu.VMEM),
        scratch_shapes=[
            store, store, store,
            pltpu.VMEM((LEV - 1, RHS, W), jnp.float32),
            pltpu.VMEM((LEV - 1, NY, SHARE, W), jnp.float32),
            pltpu.VMEM((RHS, W), jnp.float32),
            pltpu.VMEM((LEV, SHARE, W), jnp.float32),
            pltpu.VMEM((LEV - 1, BPD, W, W), jnp.bfloat16),
            pltpu.VMEM((LEV, W, W), jnp.bfloat16),
            pltpu.VMEM((LEV - 2, SHARE, W), jnp.bfloat16),
            dma((3 + 2 * LEV,)),
            dma((LEV - 1, NY)), dma((LEV - 1, NY)),
            dma((LEV - 2,)), dma((LEV - 2, NY)),
            dma((LEV - 1, NZ)), dma((LEV - 1, 2)),
            dma((LEV - 1, NX, 2)), dma((LEV - 1, NX, 2)),
            dma((LEV - 1, 8)), dma((LEV - 1, 8)),
        ],
        compiler_params=pltpu.CompilerParams(collective_id=0, has_side_effects=True),
        name="levels",
    )(
        source_ids.reshape((LEV - 1) * BPD),
        block_counts.reshape(LEV - 1),
        right_sides,
        factor_blocks,
        diag_inverses,
    )
    return out[:, None]


def solution(mesh):
    return jax.shard_map(
        shards,
        mesh=mesh,
        in_specs=(
            P(None, "rows", None, None),
            P(None, "rows", "cols", None, None, None),
            P(None, "rows", None, None),
            P(None, "rows", "cols", None),
            P(None, "rows", "cols"),
        ),
        out_specs=P(None, "rows", "cols", None),
        check_vma=False,
    )
```

time: 464 us -> 79.7 us (0.17); the launches traced: 458 us -> 79.5 us
  waiting for transfers between devices: 209 us -> 0 us
  blocking collectives: 172 us -> 0 us
  Pallas kernels: 0 us -> 76.7 us
  loops' own time: 22 us -> 0 us
  starting transfers between devices: 15.8 us -> 0 us
  between operations: 13.3 us -> 0.01 us
  local copies, waits for them, and re-layouts: 14.4 us -> 2.07 us
  matrix products: 9.78 us -> 0 us
    all_gather x3 -> x0, blocking collectives: 172 us -> none  [shards(): lax.all_gather(own_solution.astype(jnp.bfloat16)[None], 'rows', axis=0, t...]
    reduce_scatter x3 -> x0, waiting for transfers between devices: 160 us -> none  [shards(): lax.psum_scatter(partials[level_index], 'cols', scatter_dimension=0, tile...]
    pallas_call x0 -> x1, Pallas kernels: none -> 76.7 us  [shards(): pl.pallas_call(kernel, out_shape=jax.ShapeDtypeStruct((LEV, SHARE, W), jn...]
    all_to_all x3 -> x0, waiting for transfers between devices: 49.1 us -> none  [shards(): lax.all_to_all(grouped, 'cols', split_axis=1, concat_axis=2, tiled=True)]
    another operation x3 -> x0, loops' own time: 22 us -> none  [slot_sum(): return lax.fori_loop(0, live_count, add_block, running)]
    all_to_all x3 -> x0, starting transfers between devices: 15.7 us -> none  [shards(): lax.all_to_all(grouped, 'cols', split_axis=1, concat_axis=2, tiled=True)]
    dot_general x10 -> x0, matrix products: 9.78 us -> none  [the longest x6 5.56 us: add_block(): jnp.dot(solved_piece, factor_piece, preferred_element_type=jnp.float32)]
  transfers between devices with their start and end apart: 6 -> 0, of which waited for: 6 -> 0; matrix products, arithmetic and copies ran while one was open for 1% -> 0% of each run, Pallas kernels for 0% -> 0%
where the time goes in v1:
time: 79.7 us; the launch traced here: 79.5 us
  Pallas kernels  76.7 us (96%)
  local copies, waits for them, and re-layouts  2.07 us (3%)
    pallas_call x1, Pallas kernels, shards(): pl.pallas_call(kernel, out_shape=jax.ShapeDtypeStruct((LEV, SHARE, W), jn...  76.7 us

profile of v1, /device:TPU:1, one launch (start us, length us, event | category | flops | bytes accessed | tf_op | source)
XLA Modules:
  0.0 79.5 jit_solution(9586224988040952180)
XLA Ops:
  0.0 0.7 reduce
  0.7 0.6 reshape.6.ids_ref
  1.3 76.7 %levels.1 = f32[4,16,256]{2,1,0:T(8,128)} custom-call(s32[24]{0:T(128)} %reshape.6.ids_ref, s32[3]{0:T(128)} %bitcast.5, f32[4,1,128,256]{3,2,1,0:T(8,128)} %rhs_hbm.1, bf16[3,1,1,8,256,256]{5,4,3,2,1,0:T(8,128)(2,1)} %fac_hbm.1, bf16[4,1,256,256]{3,2,1,0:T(8,128)(2,1)} %diag_hbm.1), custom_call_target="tpu_custom_call" | custom-call | tf_op jit(solution)/shard_map/levels/pallas_call | solution.py:244
  78.0 1.5 %copy.8 = f32[4,1,16,256]{3,2,1,0:T(8,128)} copy(f32[4,1,16,256]{3,2,1,0:T(8,128)} %bitcast.4) | data formatting | bytes 131072

commit v2 on v0

v2 whole, which is shorter than its diff:
```python
import jax
import jax.numpy as jnp
from jax import lax
from jax.experimental import pallas as pl
from jax.experimental.pallas import tpu as pltpu
from jax.sharding import PartitionSpec as P

LEV, NX, NZ, NC, NY = 4, 4, 8, 2, 8
W, RHS, BPD = 256, 128, 8
SHARE = RHS // NY
FAR8 = (4, 3, 5, 2, 6, 1, 7)
FAR4 = (2, 1, 3)
NCH = 1
CHUNK = [pl.ds(i * (RHS // NCH), RHS // NCH) for i in range(NCH)]
MESH = pl.DeviceIdType.MESH


def kernel(
    ids_ref, counts_ref, rhs_hbm, fac_hbm, diag_hbm, out_ref,
    store0, store1, store2, part, part16, landed, last, solbuf, obuf, rhs_full, rhs_own, fac, diag,
    load_sem, r_send, r_recv, l_send, l_recv, o_send, o_recv,
    b_send, b_recv, e_send, e_recv, x_send, x_recv, c_send, c_recv, d_send, d_recv,
):
    stores = (store0, store1, store2)
    row = lax.axis_index("rows")
    col = lax.axis_index("cols")
    x = row // (NZ * NC)
    z = (row // NC) % NZ
    core = row % NC
    root = row % NY
    src_core = col % NC
    in_lane = core == src_core
    is_root = root == col
    not_root = jnp.logical_not(is_root)
    own_half = z // (NZ // 2)
    own_slot = 2 * x + own_half
    across = (x + NX // 2) % NX

    def rows_of(xx, zz, cc):
        return (xx * NZ + zz) * NC + cc

    def share(c):
        return pl.ds(pl.multiple_of(c * SHARE, SHARE), SHARE)

    def send(src, dst, send_sem, recv_sem, r, c):
        return pltpu.make_async_remote_copy(src, dst, send_sem, recv_sem, device_id=(r, c), device_id_type=MESH)

    loads = [
        pltpu.make_async_copy(rhs_hbm.at[0, 0], rhs_full.at[0], load_sem.at[0]),
        pltpu.make_async_copy(diag_hbm.at[0, 0], diag.at[0], load_sem.at[1]),
        pltpu.make_async_copy(rhs_hbm.at[:, 0, share(col), :], rhs_own, load_sem.at[2]),
    ]
    for level in range(1, LEV):
        loads.append(
            pltpu.make_async_copy(fac_hbm.at[level - 1, 0, 0], fac.at[level - 1], load_sem.at[1 + 2 * level])
        )
        loads.append(pltpu.make_async_copy(diag_hbm.at[level, 0], diag.at[level], load_sem.at[2 + 2 * level]))
    for level in range(1, LEV - 1):
        loads.append(
            pltpu.make_async_copy(rhs_hbm.at[level, 0], rhs_full.at[level], load_sem.at[2 + 2 * (LEV - 1) + level])
        )
    for copy in loads:
        copy.start()

    barrier = pltpu.get_barrier_semaphore()
    for d in FAR8:
        pl.semaphore_signal(barrier, device_id=(row, (col + d) % NY), device_id_type=MESH)
        pl.semaphore_signal(barrier, device_id=(rows_of(x, (z + d) % NZ, core), col), device_id_type=MESH)
    for d in FAR4:
        pl.semaphore_signal(barrier, device_id=(rows_of((x + d) % NX, z, core), col), device_id_type=MESH)
    pl.semaphore_signal(barrier, device_id=(rows_of(x, z, 1 - core), col), device_id_type=MESH)

    def l_copy(d):
        to = (col + d) % NY
        return send(part16.at[LEV - 2, share(to), :], last.at[d], l_send.at[d], l_recv.at[d], row, to)

    def r_copy(level, ch, d):
        return send(
            part16.at[level - 1, CHUNK[ch], :],
            landed.at[level - 1, d, CHUNK[ch], :],
            r_send.at[level - 1, ch],
            r_recv.at[level - 1, ch, d],
            row,
            root,
        )

    def o_copy(level, d):
        to = (col + d) % NY
        return send(
            solbuf.at[level - 1, share(to), :], obuf.at[level - 1], o_send.at[level - 1, d], o_recv.at[level - 1], row, to
        )

    def block(level, slot, ch):
        return stores[level].at[slot, CHUNK[ch], :]

    def b_copy(level, ch, half, d):
        ref = block(level, 2 * x + half, ch)
        return send(ref, ref, b_send.at[level, ch, d], b_recv.at[level, ch, half], rows_of(x, (z + d) % NZ, core), col)

    def e_copy(level, ch, half, d):
        ref = block(level, 2 * across + half, ch)
        return send(ref, ref, e_send.at[level, ch, d], e_recv.at[level, ch, half], rows_of(x, (z + d) % NZ, core), col)

    def x_copy(level, ch, from_x):
        ref = block(level, 2 * from_x + own_half, ch)
        return send(ref, ref, x_send.at[level, ch], x_recv.at[level, ch], rows_of(across, z, core), col)

    def c_copy(level, ch, from_x, half, d):
        ref = block(level, 2 * from_x + half, ch)
        i = (d - 1) // 2
        to = rows_of((x + d) % NX, z, core)
        return send(ref, ref, c_send.at[level, ch, half, i], c_recv.at[level, ch, half, i], to, col)

    def d_copy(level, ch, slot):
        ref = block(level, slot, ch)
        return send(ref, ref, d_send.at[level, ch, slot], d_recv.at[level, ch, slot], rows_of(x, z, 1 - core), col)

    def beside(level, ch, half):
        for d in (1, 3):
            c_copy(level, ch, x, half, d).start()

    def launch(level, ch):
        x_copy(level, ch, x).start()
        for d in FAR8:
            b_copy(level, ch, own_half, d).start()
        d_copy(level, ch, own_slot).start()

    def spread(level):
        other = 1 - own_half

        @pl.when(is_root)
        def _():
            for ch in range(NCH):
                x_copy(level, ch, across).wait_recv()
                for d in FAR8:
                    e_copy(level, ch, own_half, d).start()
                beside(level, ch, own_half)
                d_copy(level, ch, 2 * across + own_half).start()
            if level > 0:
                for d in FAR8:
                    o_copy(level, d).start()
            for ch in range(NCH):
                b_copy(level, ch, other, 1).wait_recv()
                beside(level, ch, other)
                d_copy(level, ch, 2 * x + other).start()
            for ch in range(NCH):
                e_copy(level, ch, other, 1).wait_recv()
                d_copy(level, ch, 2 * across + other).start()

        @pl.when(jnp.logical_and(in_lane, not_root))
        def _():
            for ch in range(NCH):
                for half in range(2):
                    b_copy(level, ch, half, 1).wait_recv()
                    beside(level, ch, half)
                    d_copy(level, ch, 2 * x + half).start()
            for ch in range(NCH):
                for half in range(2):
                    e_copy(level, ch, half, 1).wait_recv()
                    d_copy(level, ch, 2 * across + half).start()

        @pl.when(in_lane)
        def _():
            for ch in range(NCH):
                for half in range(2):
                    for d in (1, 3):
                        from_x = (x + NX - d) % NX
                        c_copy(level, ch, from_x, half, d).wait_recv()
                        d_copy(level, ch, 2 * from_x + half).start()

        @pl.when(jnp.logical_not(in_lane))
        def _():
            for ch in range(NCH):
                for slot in range(8):
                    d_copy(level, ch, slot).wait_recv()

    def drain(level):
        if level == LEV - 1:
            for d in FAR8:
                l_copy(d).wait_send()
            return
        if level > 0:

            @pl.when(not_root)
            def _():
                for ch in range(NCH):
                    r_copy(level, ch, 1).wait_send()

        @pl.when(is_root)
        def _():
            if level > 0:
                for d in FAR8:
                    o_copy(level, d).wait_send()
            for ch in range(NCH):
                x_copy(level, ch, x).wait_send()
                for d in FAR8:
                    b_copy(level, ch, own_half, d).wait_send()
                    e_copy(level, ch, own_half, d).wait_send()

        @pl.when(in_lane)
        def _():
            for ch in range(NCH):
                for half in range(2):
                    for d in (1, 3):
                        c_copy(level, ch, x, half, d).wait_send()
                for slot in range(8):
                    d_copy(level, ch, slot).wait_send()

    loads[0].wait()
    loads[1].wait()

    @pl.when(is_root)
    def _():
        whole = jnp.dot(rhs_full[0].astype(jnp.bfloat16), diag[0], preferred_element_type=jnp.float32)
        store0[own_slot] = whole.astype(jnp.bfloat16)

    loads[2].wait()
    out_ref[0] = jnp.dot(rhs_own[0].astype(jnp.bfloat16), diag[0], preferred_element_type=jnp.float32)
    pl.semaphore_wait(barrier, 2 * (NY - 1) + NX)

    @pl.when(is_root)
    def _():
        for ch in range(NCH):
            launch(0, ch)

    for copy in loads[3:]:
        copy.wait()
    spread(0)

    for level in range(1, LEV):
        live = counts_ref[level - 1]
        total = jnp.zeros((RHS, W), jnp.float32)
        for k in range(BPD):
            source = ids_ref[level - 1, 0, 0, k]
            place = (source % (NX * NZ * NC)) // NY
            held = source // (NX * NZ * NC)
            chosen = store0[place]
            for m in range(1, level):
                chosen = lax.select(held == m, stores[m][place], chosen)
            chosen = lax.select(k < live, chosen, jnp.zeros_like(chosen))
            total = total + jnp.dot(chosen, fac[level - 1, k], preferred_element_type=jnp.float32)
        part[...] = total
        part16[level - 1] = total.astype(jnp.bfloat16)
        if level == LEV - 1:
            break

        @pl.when(not_root)
        def _():
            d = (col + NY - root) % NY
            for ch in range(NCH):
                r_copy(level, ch, d).start()

        @pl.when(is_root)
        def _():
            for ch in range(NCH):
                update = part[CHUNK[ch], :]
                for d in (1, 7, 2, 6, 3, 5, 4):
                    r_copy(level, ch, d).wait_recv()
                    update = update + landed[level - 1, d, CHUNK[ch], :].astype(jnp.float32)
                reduced = (rhs_full[level, CHUNK[ch], :] - update).astype(jnp.bfloat16)
                solved = jnp.dot(reduced, diag[level], preferred_element_type=jnp.float32)
                stores[level][own_slot, CHUNK[ch], :] = solved.astype(jnp.bfloat16)
                solbuf[level - 1, CHUNK[ch], :] = solved
                launch(level, ch)

        spread(level)

    for d in FAR8:
        l_copy(d).start()
    for level in range(1, LEV - 1):

        @pl.when(is_root)
        def _():
            out_ref[level] = solbuf[level - 1, share(col), :]

        @pl.when(not_root)
        def _():
            o_copy(level, 1).wait_recv()
            out_ref[level] = obuf[level - 1]

    for level in range(LEV - 1):
        drain(level)
    update = part[share(col), :]
    for d in (1, 7, 2, 6, 3, 5, 4):
        l_copy(d).wait_recv()
        update = update + last[d].astype(jnp.float32)
    reduced = (rhs_own[LEV - 1] - update).astype(jnp.bfloat16)
    out_ref[LEV - 1] = jnp.dot(reduced, diag[LEV - 1], preferred_element_type=jnp.float32)
    drain(LEV - 1)


def shards(right_sides, factor_blocks, diag_inverses, source_ids, block_counts):
    dma = pltpu.SemaphoreType.DMA
    hbm = pl.BlockSpec(memory_space=pl.ANY)
    smem = pl.BlockSpec(memory_space=pltpu.SMEM)
    store = pltpu.VMEM((8, RHS, W), jnp.bfloat16)
    mid, spreads = LEV - 2, LEV - 1
    out = pl.pallas_call(
        kernel,
        out_shape=jax.ShapeDtypeStruct((LEV, SHARE, W), jnp.float32),
        in_specs=[smem, smem, hbm, hbm, hbm],
        out_specs=pl.BlockSpec(memory_space=pltpu.VMEM),
        scratch_shapes=[
            store, store, store,
            pltpu.VMEM((RHS, W), jnp.float32),
            pltpu.VMEM((LEV - 1, RHS, W), jnp.bfloat16),
            pltpu.VMEM((mid, NY, RHS, W), jnp.bfloat16),
            pltpu.VMEM((NY, SHARE, W), jnp.bfloat16),
            pltpu.VMEM((mid, RHS, W), jnp.float32),
            pltpu.VMEM((mid, SHARE, W), jnp.float32),
            pltpu.VMEM((LEV - 1, RHS, W), jnp.float32),
            pltpu.VMEM((LEV, SHARE, W), jnp.float32),
            pltpu.VMEM((LEV - 1, BPD, W, W), jnp.bfloat16),
            pltpu.VMEM((LEV, W, W), jnp.bfloat16),
            dma((3 * LEV,)),
            dma((mid, NCH)), dma((mid, NCH, NY)),
            dma((NY,)), dma((NY,)),
            dma((mid, NY)), dma((mid,)),
            dma((spreads, NCH, NZ)), dma((spreads, NCH, 2)),
            dma((spreads, NCH, NZ)), dma((spreads, NCH, 2)),
            dma((spreads, NCH)), dma((spreads, NCH)),
            dma((spreads, NCH, 2, 2)), dma((spreads, NCH, 2, 2)),
            dma((spreads, NCH, 8)), dma((spreads, NCH, 8)),
        ],
        compiler_params=pltpu.CompilerParams(collective_id=0, has_side_effects=True),
        name="levels",
    )(source_ids, block_counts.reshape(LEV - 1), right_sides, factor_blocks, diag_inverses)
    return out[:, None]


def solution(mesh):
    return jax.shard_map(
        shards,
        mesh=mesh,
        in_specs=(
            P(None, "rows", None, None),
            P(None, "rows", "cols", None, None, None),
            P(None, "rows", None, None),
            P(None, "rows", "cols", None),
            P(None, "rows", "cols"),
        ),
        out_specs=P(None, "rows", "cols", None),
        check_vma=False,
    )
```

time: 464 us -> 67.5 us (0.15); the launches traced: 458 us -> 67.3 us
  waiting for transfers between devices: 209 us -> 0 us
  blocking collectives: 172 us -> 0 us
  Pallas kernels: 0 us -> 65.8 us
  loops' own time: 22 us -> 0 us
  starting transfers between devices: 15.8 us -> 0 us
  between operations: 13.3 us -> 0.01 us
  local copies, waits for them, and re-layouts: 14.4 us -> 1.47 us
  matrix products: 9.78 us -> 0 us
    all_gather x3 -> x0, blocking collectives: 172 us -> none  [shards(): lax.all_gather(own_solution.astype(jnp.bfloat16)[None], 'rows', axis=0, t...]
    reduce_scatter x3 -> x0, waiting for transfers between devices: 160 us -> none  [shards(): lax.psum_scatter(partials[level_index], 'cols', scatter_dimension=0, tile...]
    pallas_call x0 -> x1, Pallas kernels: none -> 65.8 us  [shards(): pl.pallas_call(kernel, out_shape=jax.ShapeDtypeStruct((LEV, SHARE, W), jn...]
    all_to_all x3 -> x0, waiting for transfers between devices: 49.1 us -> none  [shards(): lax.all_to_all(grouped, 'cols', split_axis=1, concat_axis=2, tiled=True)]
    another operation x3 -> x0, loops' own time: 22 us -> none  [slot_sum(): return lax.fori_loop(0, live_count, add_block, running)]
    all_to_all x3 -> x0, starting transfers between devices: 15.7 us -> none  [shards(): lax.all_to_all(grouped, 'cols', split_axis=1, concat_axis=2, tiled=True)]
    dot_general x10 -> x0, matrix products: 9.78 us -> none  [the longest x6 5.56 us: add_block(): jnp.dot(solved_piece, factor_piece, preferred_element_type=jnp.float32)]
  transfers between devices with their start and end apart: 6 -> 0, of which waited for: 6 -> 0; matrix products, arithmetic and copies ran while one was open for 1% -> 0% of each run, Pallas kernels for 0% -> 0%
where the time goes in v2:
time: 67.5 us; the launch traced here: 67.3 us
  Pallas kernels  65.8 us (97%)
  local copies, waits for them, and re-layouts  1.47 us (2%)
    pallas_call x1, Pallas kernels, shards(): pl.pallas_call(kernel, out_shape=jax.ShapeDtypeStruct((LEV, SHARE, W), jn...  65.8 us
    unnamed x1, local copies, waits for them, and re-layouts  1.47 us

profile of v2, /device:TPU:1, one launch (start us, length us, event | category | flops | bytes accessed | tf_op | source)
XLA Modules:
  0.0 67.3 jit_solution(5437216923169518764)
XLA Ops:
  0.0 65.8 %levels.1 = f32[4,16,256]{2,1,0:T(8,128)} custom-call(s32[3,1,1,8]{3,2,1,0:T(1,128)} %ids_ref.1, s32[3]{0:T(128)} %bitcast.5, f32[4,1,128,256]{3,2,1,0:T(8,128)} %rhs_hbm.1, bf16[3,1,1,8,256,256]{5,4,3,2,1,0:T(8,128)(2,1)} %fac_hbm.1, bf16[4,1,256,256]{3,2,1,0:T(8,128)(2,1)} %diag_hbm.1), custom_call_target="tpu_custom_call" | custom-call | tf_op jit(solution)/shard_map/levels/pallas_call | solution.py:298
  65.8 1.5 %copy.8 = f32[4,1,16,256]{3,2,1,0:T(8,128)} copy(f32[4,1,16,256]{3,2,1,0:T(8,128)} %bitcast.4) | data formatting | bytes 131072

commit v3 on v2

--- a/solution.py
+++ b/solution.py
@@ -8,7 +8,7 @@
 LEV, NX, NZ, NC, NY = 4, 4, 8, 2, 8
 W, RHS, BPD = 256, 128, 8
 SHARE = RHS // NY
-FAR8 = (4, 3, 5, 2, 6, 1, 7)
+FAR8 = (5, 3, 6, 2, 7, 1, 4)
 FAR4 = (2, 1, 3)
 NCH = 1
 CHUNK = [pl.ds(i * (RHS // NCH), RHS // NCH) for i in range(NCH)]
@@ -263,6 +263,7 @@
                 solbuf[level - 1, CHUNK[ch], :] = solved
                 launch(level, ch)
 
+        drain(level - 1)
         spread(level)
 
     for d in FAR8:
@@ -278,8 +279,7 @@
             o_copy(level, 1).wait_recv()
             out_ref[level] = obuf[level - 1]
 
-    for level in range(LEV - 1):
-        drain(level)
+    drain(LEV - 2)
     update = part[share(col), :]
     for d in (1, 7, 2, 6, 3, 5, 4):
         l_copy(d).wait_recv()

time: 67.5 us -> 66.3 us (0.982)
  Pallas kernels: 65.8 us -> 64.7 us
    pallas_call x1, Pallas kernels: 65.8 us -> 64.7 us  [shards(): pl.pallas_call(kernel, out_shape=jax.ShapeDtypeStruct((LEV, SHARE, W), jn...]
where the time goes in v3:
time: 66.3 us; the launch traced here: 66.2 us
  Pallas kernels  64.7 us (98%)
  local copies, waits for them, and re-layouts  1.47 us (2%)
    pallas_call x1, Pallas kernels, shards(): pl.pallas_call(kernel, out_shape=jax.ShapeDtypeStruct((LEV, SHARE, W), jn...  64.7 us
    unnamed x1, local copies, waits for them, and re-layouts  1.47 us

profile of v3, /device:TPU:1, one launch (start us, length us, event | category | flops | bytes accessed | tf_op | source)
XLA Modules:
  0.0 66.2 jit_solution(102033694991684600)
XLA Ops:
  0.0 64.7 %levels.1 = f32[4,16,256]{2,1,0:T(8,128)} custom-call(s32[3,1,1,8]{3,2,1,0:T(1,128)} %ids_ref.1, s32[3]{0:T(128)} %bitcast.5, f32[4,1,128,256]{3,2,1,0:T(8,128)} %rhs_hbm.1, bf16[3,1,1,8,256,256]{5,4,3,2,1,0:T(8,128)(2,1)} %fac_hbm.1, bf16[4,1,256,256]{3,2,1,0:T(8,128)(2,1)} %diag_hbm.1), custom_call_target="tpu_custom_call" | custom-call | tf_op jit(solution)/shard_map/levels/pallas_call | solution.py:298
  64.7 1.5 %copy.8 = f32[4,1,16,256]{3,2,1,0:T(8,128)} copy(f32[4,1,16,256]{3,2,1,0:T(8,128)} %bitcast.4) | data formatting | bytes 131072

commit v4 on v3

--- a/solution.py
+++ b/solution.py
@@ -143,9 +143,6 @@
                 b_copy(level, ch, other, 1).wait_recv()
                 beside(level, ch, other)
                 d_copy(level, ch, 2 * x + other).start()
-            for ch in range(NCH):
-                e_copy(level, ch, other, 1).wait_recv()
-                d_copy(level, ch, 2 * across + other).start()
 
         @pl.when(jnp.logical_and(in_lane, not_root))
         def _():
@@ -154,10 +151,6 @@
                     b_copy(level, ch, half, 1).wait_recv()
                     beside(level, ch, half)
                     d_copy(level, ch, 2 * x + half).start()
-            for ch in range(NCH):
-                for half in range(2):
-                    e_copy(level, ch, half, 1).wait_recv()
-                    d_copy(level, ch, 2 * across + half).start()
 
         @pl.when(in_lane)
         def _():
@@ -167,6 +160,19 @@
                         from_x = (x + NX - d) % NX
                         c_copy(level, ch, from_x, half, d).wait_recv()
                         d_copy(level, ch, 2 * from_x + half).start()
+
+        @pl.when(is_root)
+        def _():
+            for ch in range(NCH):
+                e_copy(level, ch, other, 1).wait_recv()
+                d_copy(level, ch, 2 * across + other).start()
+
+        @pl.when(jnp.logical_and(in_lane, not_root))
+        def _():
+            for ch in range(NCH):
+                for half in range(2):
+                    e_copy(level, ch, half, 1).wait_recv()
+                    d_copy(level, ch, 2 * across + half).start()
 
         @pl.when(jnp.logical_not(in_lane))
         def _():
@@ -239,8 +245,11 @@
                 chosen = lax.select(held == m, stores[m][place], chosen)
             chosen = lax.select(k < live, chosen, jnp.zeros_like(chosen))
             total = total + jnp.dot(chosen, fac[level - 1, k], preferred_element_type=jnp.float32)
+        part16[level - 1] = total.astype(jnp.bfloat16)
+        if level == LEV - 1:
+            for d in FAR8:
+                l_copy(d).start()
         part[...] = total
-        part16[level - 1] = total.astype(jnp.bfloat16)
         if level == LEV - 1:
             break
 
@@ -266,8 +275,6 @@
         drain(level - 1)
         spread(level)
 
-    for d in FAR8:
-        l_copy(d).start()
     for level in range(1, LEV - 1):
 
         @pl.when(is_root)

time: 66.3 us -> 66.1 us (level)
  no operation moved by 1% of the time
where the time goes in v4:
time: 66.1 us; the launch traced here: 65.9 us
  Pallas kernels  64.5 us (98%)
  local copies, waits for them, and re-layouts  1.47 us (2%)
    pallas_call x1, Pallas kernels, shards(): pl.pallas_call(kernel, out_shape=jax.ShapeDtypeStruct((LEV, SHARE, W), jn...  64.5 us
    unnamed x1, local copies, waits for them, and re-layouts  1.47 us

profile of v4, /device:TPU:1, one launch (start us, length us, event | category | flops | bytes accessed | tf_op | source)
XLA Modules:
  0.0 65.9 jit_solution(6581895673682235331)
XLA Ops:
  0.0 64.5 %levels.1 = f32[4,16,256]{2,1,0:T(8,128)} custom-call(s32[3,1,1,8]{3,2,1,0:T(1,128)} %ids_ref.1, s32[3]{0:T(128)} %bitcast.5, f32[4,1,128,256]{3,2,1,0:T(8,128)} %rhs_hbm.1, bf16[3,1,1,8,256,256]{5,4,3,2,1,0:T(8,128)(2,1)} %fac_hbm.1, bf16[4,1,256,256]{3,2,1,0:T(8,128)(2,1)} %diag_hbm.1), custom_call_target="tpu_custom_call" | custom-call | tf_op jit(solution)/shard_map/levels/pallas_call | solution.py:305
  64.5 1.5 %copy.8 = f32[4,1,16,256]{3,2,1,0:T(8,128)} copy(f32[4,1,16,256]{3,2,1,0:T(8,128)} %bitcast.4) | data formatting | bytes 131072
